TPU v7x, 32 devices: a whole 2x2x4 slice. The times are simulated.
32 devices in a mesh: section: 8 (over y, x, core), rep: 4 (over z).
Axes of the slice: x: 2, y: 2, z: 4, core: 2. Of those that a mesh axis runs over, the one named last changes fastest.
Arguments:
- features: bfloat16 [16384, 128], P('section'), may hold values from -6 to 6
- order: int32 [16384], P('section'), may hold values from 0 to 2047, as said below
- tiles: bfloat16 [8, 4, 2, 96, 128, 128], P('section', 'rep'), may hold values from -0.125 to 0.125
- tile_rows: int32 [8, 4, 2, 96], P('section', 'rep'), may hold values from 0 to 15, as said below
- tile_cols: int32 [8, 4, 2, 96], P('section', 'rep'), may hold values from 0 to 15, as said below
- live: int32 [8, 4, 2], P('section', 'rep'), may hold values from 1 to 96, as said below
- weight: bfloat16 [128, 128], replicated, may hold values from -0.5 to 0.5
- cotangent: bfloat16 [16384, 128], P('section'), may hold values from -6 to 6
Outputs:
- hidden: bfloat16 [16384, 128], P('section')
- weight_grad: float32 [128, 128], replicated
- feature_grad: bfloat16 [16384, 128], P('section')
Inputs may be any that keep to these rules, and one draw needn't show every extreme that they name: `order`: within each panel of 2048 rows, a permutation of the local row numbers. For one section, replica and round, the 96 pairs (tile_rows, tile_cols) are distinct. `tile_cols`: block column within the panel j * 4 + r for replica r and round j. Some section, replica and round has all 96 slots live.
All inputs are finite; a program needn't handle non-finite values.
Results may differ from a plain program's by a relative error of at most 0.012.
Values may be sent and summed in bfloat16 or wider, within the bound.
No kernel may reach another device: no remote copies, remote signals or barrier semaphores. Data moves between devices by JAX's collectives and lax.ppermute only.
A program may use at most 192 MiB of HBM per device.

v0:
```python
import math
import jax
import jax.numpy as jnp
from jax import lax
from jax.sharding import PartitionSpec as P


def spread(value, axis, source):
    kept = jnp.where(lax.axis_index(axis) == source, value, 0).astype(value.dtype)
    return lax.psum(kept, axis)


def shards(features, order, tiles, tile_rows, tile_cols, live, weight, cotangent):
    rep_count = lax.axis_size("rep")
    section_count = lax.axis_size("section")
    rep_index = lax.axis_index("rep")
    section_index = lax.axis_index("section")
    panel_rows, width = features.shape
    block_rows = tiles.shape[-1]
    blocks = panel_rows // block_rows
    rounds = tiles.shape[2]
    slot_count = tiles.shape[3]
    own_tiles = tiles[0, 0]
    row_table = tile_rows[0, 0]
    col_table = tile_cols[0, 0]
    live_counts = live[0, 0]
    slot_ids = jnp.arange(slot_count, dtype=jnp.int32)
    block_ids = jnp.arange(blocks, dtype=jnp.int32)
    grad_scale = 1.0 / math.sqrt(panel_rows * section_count)
    reordered = jnp.take(features, order, axis=0)

    def forward_round(round_no, running):
        root = round_no * rep_count + rep_index
        panel = spread(reordered, "section", root)
        tile_set = lax.dynamic_index_in_dim(own_tiles, round_no, 0, keepdims=False)
        row_ids = lax.dynamic_index_in_dim(row_table, round_no, 0, keepdims=False)
        col_ids = lax.dynamic_index_in_dim(col_table, round_no, 0, keepdims=False)
        count_now = lax.dynamic_index_in_dim(live_counts, round_no, 0, keepdims=False)
        picked = jnp.take(panel.reshape(blocks, block_rows, width), col_ids, axis=0)
        products = jnp.einsum("kab,kbf->kaf", tile_set, picked, preferred_element_type=jnp.float32)
        select = (
            (row_ids[None, :] == block_ids[:, None]) & (slot_ids < count_now)[None, :]
        ).astype(jnp.float32)
        return running + jnp.einsum(
            "pk,kaf->paf", select, products, precision=lax.Precision.HIGHEST
        )

    partial_sum = lax.fori_loop(
        0, rounds, forward_round, jnp.zeros((blocks, block_rows, width), jnp.float32)
    )
    partial_sum = partial_sum.reshape(panel_rows, width)
    share_rows = panel_rows // rep_count
    row_share = lax.psum_scatter(partial_sum, "rep", scatter_dimension=0, tiled=True)
    co_share = lax.dynamic_slice_in_dim(cotangent, rep_index * share_rows, share_rows, 0)
    aggregated = row_share.astype(jnp.bfloat16)
    preact = jnp.dot(aggregated, weight, preferred_element_type=jnp.float32)
    out_rows = jax.nn.silu(preact).astype(jnp.bfloat16)
    sigmoid_part = jax.nn.sigmoid(preact)
    grad_pre = (
        co_share.astype(jnp.float32) * sigmoid_part * (1.0 + preact * (1.0 - sigmoid_part))
    ).astype(jnp.bfloat16)
    grad_part = jnp.einsum("nf,ng->fg", aggregated, grad_pre, preferred_element_type=jnp.float32)
    up_rows = jnp.einsum("ng,fg->nf", grad_pre, weight, preferred_element_type=jnp.float32).astype(
        jnp.bfloat16
    )
    hidden_share, grad_part, upstream_share = (out_rows, grad_part, up_rows)
    weight_grad = lax.psum(grad_part, ("section", "rep")) * grad_scale
    hidden, upstream = (
        lax.all_gather(hidden_share, "rep", axis=0, tiled=True),
        lax.all_gather(upstream_share, "rep", axis=0, tiled=True),
    )
    up_blocks = upstream.reshape(blocks, block_rows, width)
    picked_up = jnp.take(up_blocks, row_table.reshape(-1), axis=0).reshape(
        rounds, slot_count, block_rows, width
    )
    products_back = jnp.einsum(
        "jkab,jkaf->jkbf", own_tiles, picked_up, preferred_element_type=jnp.float32
    )
    alive_mask = slot_ids[None, None, :] < live_counts[:, None, None]
    select_back = ((col_table[:, None, :] == block_ids[None, :, None]) & alive_mask).astype(
        jnp.float32
    )
    contrib = jnp.einsum(
        "jpk,jkbf->jpbf", select_back, products_back, precision=lax.Precision.HIGHEST
    )
    contrib = lax.optimization_barrier(contrib.astype(jnp.bfloat16)).astype(jnp.float32)
    contrib = contrib.reshape(rounds, panel_rows, width)
    totals = lax.psum(contrib.astype(jnp.bfloat16), "section").astype(jnp.float32)
    own_panel = lax.dynamic_index_in_dim(
        totals, section_index // rep_count, 0, keepdims=False
    ).astype(jnp.bfloat16)
    grad_rows = spread(own_panel, "rep", section_index % rep_count)
    feature_grad = jnp.zeros_like(features).at[order].set(grad_rows)
    return (hidden, weight_grad, feature_grad)


def solution(mesh):
    placed = (
        P("section", None),
        P("section"),
        P("section", "rep", None, None, None, None),
        P("section", "rep", None, None),
        P("section", "rep", None, None),
        P("section", "rep", None),
        P(),
        P("section", None),
    )
    return jax.shard_map(
        shards,
        mesh=mesh,
        in_specs=placed,
        out_specs=(P("section", None), P(), P("section", None)),
        check_vma=False,
    )
```

profile of v0, /device:TPU:0, one launch (start us, length us, event | category | flops | bytes accessed | tf_op | source)
XLA Modules:
  0.0 487.0 jit_solution(13288153377587932532)
XLA Ops:
  9.5 6.2 %gather_fusion.1 = bf16[2048,128]{1,0:T(8,128)(2,1)S(1)} fusion(bf16[2048,128]{1,0:T(8,128)(2,1)S(1)} %copy-done, s32[2048]{0:T(1024)S(1)} %get-tuple-element.296), kind=kCustom, calls=%fused_computation.1 | custom fusion | bytes 1056768 | tf_op jit(solution)/shard_map/jit(_take)/gather | solution.py:30
  16.0 147.6 %while.16 = (s32[]{:T(128)}, f32[16,128,128]{2,0,1:T(8,128)S(1)}, s32[2,96]{1,0:T(2,128)}, s32[2]{0:T(128)}, bf16[2,96,128,128]{3,2,1,0:T(8,128)(2,1)}, /*index=...) while((s32[]{:T(128)}, f32[16,128,128]{2,0,1:T(8,128)S(1)}, ...), condition=%wide.region_2.3_spmd.clone, body=%wide.region_0.0_spmd.clone.sunk | while | flops 707269568 | bytes 31465112 | solution.py:48
  16.1 0.8 broadcast_select_fusion.3
  18.3 1.2 dynamic_slice.80
  20.9 57.2 %all-reduce.11.cloned.1.call-done = bf16[16,128,128]{2,1,0:T(8,128)(2,1)} async-done(((bf16[16,128,128]{2,1,0:T(8,128)(2,1)}), bf16[16,128,128]{2,1,0:T(8,128)(2,1)}) %all-reduce.11.cloned.1.call-update) | async-done | bytes 524304 | tf_op jit(solution)/shard_map/while/body/eval_jaxpr/psum | solution.py:10
  78.1 3.7 gather_fusion
  81.9 3.9 fusion.65
  85.8 5.7 %fusion.67 = f32[16,128,128]{2,0,1:T(8,128)S(1)} fusion(f32[96,128,128]{2,1,0:T(8,128)S(1)} %fusion.65, f32[16,128,128]{2,0,1:T(8,128)S(1)} %get-tuple-element.360, pred[]{:T(512)S(6)} %compare.6, s32[96]{0:T(128)S(1)} %fusion.66, pred[96]{0:T(512)(128)(4,1)S(1)} %iota_compare_fusion.5), kind=kOutput, calls=%fused_computation.14.clone.1 | convolution fusion | flops 302517248 | bytes 8389089 | tf_op jit(solution)/shard_map/while/body/eval_jaxpr/pk,kaf->paf/dot_general | solution.py:44
  91.6 0.8 broadcast_select_fusion.3
  93.8 1.2 dynamic_slice.80
  96.4 53.8 %all-reduce.11.cloned.1.call-done = bf16[16,128,128]{2,1,0:T(8,128)(2,1)} async-done(((bf16[16,128,128]{2,1,0:T(8,128)(2,1)}), bf16[16,128,128]{2,1,0:T(8,128)(2,1)}) %all-reduce.11.cloned.1.call-update) | async-done | bytes 524304 | tf_op jit(solution)/shard_map/while/body/eval_jaxpr/psum | solution.py:10
  150.2 3.7 gather_fusion
  154.0 3.9 fusion.65
  157.9 5.7 %fusion.67 = f32[16,128,128]{2,0,1:T(8,128)S(1)} fusion(f32[96,128,128]{2,1,0:T(8,128)S(1)} %fusion.65, f32[16,128,128]{2,0,1:T(8,128)S(1)} %get-tuple-element.360, pred[]{:T(512)S(6)} %compare.6, s32[96]{0:T(128)S(1)} %fusion.66, pred[96]{0:T(512)(128)(4,1)S(1)} %iota_compare_fusion.5), kind=kOutput, calls=%fused_computation.14.clone.1 | convolution fusion | flops 302517248 | bytes 8389089 | tf_op jit(solution)/shard_map/while/body/eval_jaxpr/pk,kaf->paf/dot_general | solution.py:44
  163.7 1.3 copy.11
  167.3 25.6 %reduce-scatter.2.cloned.1.call-done = f32[512,128]{1,0:T(8,128)} async-done(((f32[2048,128]{1,0:T(8,128)}), f32[512,128]{1,0:T(8,128)}) %reduce-scatter.2.cloned.1.call-update) | async-done | bytes 262160 | tf_op jit(solution)/shard_map/reduce_scatter | solution.py:53
  192.9 1.3 multiply_convert_fusion
  194.3 16.2 %all_gather.7 = bf16[2048,128]{1,0:T(8,128)(2,1)S(1)} all-gather(bf16[512,128]{1,0:T(8,128)(2,1)S(1)} %convolution_convert_fusion), channel_id=1, replica_groups=mesh['section'=8,'rep'=4] {'rep'}, dimensions={0}, use_global_device_ids=true | all-gather | bytes 655360 | tf_op jit(solution)/shard_map/all_gather | solution.py:70
  210.5 8.0 %gather_fusion.2 = bf16[192,128,128]{2,1,0:T(8,128)(2,1)} fusion(bf16[16,128,128]{2,1,0:T(8,128)(2,1)S(1)} %bitcast.60, s32[1024]{0:T(1024)S(1)} %pad_clamp_fusion.1), kind=kCustom, calls=%fused_computation.2 | custom fusion | bytes 12583680 | tf_op jit(solution)/shard_map/jit(_take)/gather | solution.py:73
  218.5 11.6 %fusion.26 = f32[2,96,128,128]{3,2,1,0:T(8,128)} fusion(bf16[2,96,128,128]{3,2,1,0:T(8,128)(2,1)} %bitcast.64, pred[2,96]{1,0:T(4,128)(4,1)S(1)} %compare_and_fusion.2, bf16[1,1,2,96,128,128]{5,4,3,2,1,0:T(8,128)(2,1)} %bitcast.62), kind=kOutput, calls=%fused_computation.34 | convolution fusion | flops 808452096 | bytes 25166016 | tf_op jit(solution)/shard_map/jkab,jkaf->jkbf/dot_general | solution.py:76
  230.1 12.8 %copy.14 = f32[2,96,128,128]{2,1,3,0:T(8,128)} copy(f32[2,96,128,128]{3,2,1,0:T(8,128)} %fusion.26) | data formatting | bytes 25165824 | tf_op jit(solution)/shard_map/jkab,jkaf->jkbf/dot_general | solution.py:76
  242.8 7.2 %fusion.30 = bf16[2,16,128,128]{3,1,2,0:T(8,128)(2,1)S(1)} fusion(f32[2,96,128,128]{2,1,3,0:T(8,128)} %copy.14, s32[2,96]{1,0:T(2,128)S(1)} %copy-done.3, pred[2,96]{1,0:T(4,128)(4,1)S(1)} %iota_compare_fusion.3), kind=kOutput, calls=%fused_computation.38 | convolution fusion | flops 604510208 | bytes 13632448 | tf_op jit(solution)/shard_map/jpk,jkbf->jpbf/dot_general | solution.py:83
  250.1 1.3 copy.12
  251.5 0.9 fusion.37
  252.5 53.3 %all-reduce.7.cloned.1.call-done = bf16[2,2048,128]{2,1,0:T(8,128)(2,1)} async-done(((bf16[2,2048,128]{2,1,0:T(8,128)(2,1)}), bf16[2,2048,128]{2,1,0:T(8,128)(2,1)}) %all-reduce.7.cloned.1.call-update) | async-done | bytes 1048592 | tf_op jit(solution)/shard_map/psum | solution.py:88
  305.8 1.9 fusion.34
  307.7 14.8 %all_gather.6 = bf16[2048,128]{1,0:T(8,128)(2,1)S(1)} all-gather(bf16[512,128]{1,0:T(8,128)(2,1)S(1)} %get-tuple-element.294), channel_id=1, replica_groups=mesh['section'=8,'rep'=4] {'rep'}, dimensions={0}, use_global_device_ids=true | all-gather | bytes 655360 | tf_op jit(solution)/shard_map/all_gather | solution.py:69
  322.5 106.7 %all-reduce.5.cloned.1.call-done = f32[128,128]{1,0:T(8,128)} async-done(((f32[128,128]{1,0:T(8,128)}), f32[128,128]{1,0:T(8,128)}) %all-reduce.5.cloned.1.call-update) | async-done | bytes 65552 | tf_op jit(solution)/shard_map/psum | solution.py:67
  429.3 1.5 broadcast_multiply_fusion
  430.7 41.1 %all-reduce.9.cloned.1.call-done = bf16[2048,128]{1,0:T(8,128)(2,1)} async-done(((bf16[2048,128]{1,0:T(8,128)(2,1)}), bf16[2048,128]{1,0:T(8,128)(2,1)}) %all-reduce.9.cloned.1.call-update) | async-done | bytes 524304 | tf_op jit(solution)/shard_map/psum | solution.py:10
  471.8 6.8 %scatter_custom_fusion = bf16[2048,128]{1,0:T(8,128)(2,1)} fusion(s32[2048]{0:T(1024)S(1)} %get-tuple-element.295, bf16[2048,128]{1,0:T(8,128)(2,1)} %all-reduce.9.cloned.1.call-done, bf16[]{:T(256)} %constant.190.clone.1), kind=kCustom, calls=%fused_computation.44 | custom fusion | bytes 524800 | tf_op jit(solution)/shard_map/scatter | solution.py:93
  478.7 0.8 copy.33
  (40 shorter events, 10.0 us)
Async XLA Ops:
  8.0 1.5 copy-start
  16.0 176.9 %copy-start.2 = (bf16[128,128]{1,0:T(8,128)(2,1)S(1)}, bf16[128,128]{1,0:T(8,128)(2,1)}, u32[]{:S(2)}) copy-start(bf16[128,128]{1,0:T(8,128)(2,1)} %param.16) | copy-start | bytes 98308
  16.0 62.1 %all-reduce.11.cloned.1.call-start = ((), (), s32[]{:S(2)}) async-start(), calls=%async_computation.5 | async-start | bytes 1048576 | tf_op jit(solution)/shard_map/while/body/eval_jaxpr/psum | solution.py:10
  91.5 58.7 %all-reduce.11.cloned.1.call-start = ((), (), s32[]{:S(2)}) async-start(), calls=%async_computation.5 | async-start | bytes 1048576 | tf_op jit(solution)/shard_map/while/body/eval_jaxpr/psum | solution.py:10
  163.6 29.2 %reduce-scatter.2.cloned.1.call-start = ((), (), s32[]{:S(2)}) async-start(), calls=%async_computation.1 | async-start | bytes 1310720 | tf_op jit(solution)/shard_map/reduce_scatter | solution.py:53
  165.0 140.7 %all-reduce.7.cloned.1.call-start = ((), (), s32[]{:S(2)}) async-start(), calls=%async_computation.3 | async-start | bytes 2097152 | tf_op jit(solution)/shard_map/psum | solution.py:88
  230.1 12.8 %copy-start.3 = (s32[2,96]{1,0:T(2,128)S(1)}, s32[2,96]{1,0:T(2,128)}, u32[]{:S(2)}) copy-start(s32[2,96]{1,0:T(2,128)} %get-tuple-element.411) | copy-start | bytes 2308
  242.8 8.7 %copy-start.1 = (f32[512,128]{1,0:T(8,128)S(1)}, f32[512,128]{1,0:T(8,128)}, u32[]{:S(2)}) copy-start(f32[512,128]{1,0:T(8,128)} %reduce-scatter.2.cloned.1.call-done) | copy-start | bytes 786436
  251.4 177.8 %all-reduce.5.cloned.1.call-start = ((), (), s32[]{:S(2)}) async-start(), calls=%async_computation.2 | async-start | bytes 131072 | tf_op jit(solution)/shard_map/psum | solution.py:67
  252.4 219.4 %all-reduce.9.cloned.1.call-start = ((), (), s32[]{:S(2)}) async-start(), calls=%async_computation.4 | async-start | bytes 1048576 | tf_op jit(solution)/shard_map/psum | solution.py:10
Sparse Core Ops, SparseCore 0:
  20.8 57.2 all-reduce.10
  96.3 53.8 all-reduce.10
Sparse Core Ops, SparseCore 1:
  166.4 26.4 reduce-scatter.1
  251.5 54.2 all-reduce.6
  312.7 116.5 all-reduce.4
  432.3 39.4 all-reduce.8
where the time goes:
time: 488 us; the launch traced here: 487 us
  waiting for transfers between devices  338 us (69%)
  local copies, waits for them, and re-layouts  49.3 us (10%)
  matrix products  40.4 us (8%)
  blocking collectives  31 us (6%)
  between operations  15.8 us (3%)
  other arithmetic  12.4 us (3%)
    psum x3, waiting for transfers between devices, spread(): return lax.psum(kept, axis)  152 us
    psum x1, waiting for transfers between devices, shards(): weight_grad = lax.psum(grad_part, ('section', 'rep')) * grad_scale  107 us
    psum x1, waiting for transfers between devices, shards(): lax.psum(contrib.astype(jnp.bfloat16), 'section').astype(jnp.float32)  53.3 us
    reduce_scatter x1, waiting for transfers between devices, shards(): lax.psum_scatter(partial_sum, 'rep', scatter_dimension=0, tiled=True)  25.6 us
    all_gather x1, blocking collectives, shards(): lax.all_gather(upstream_share, 'rep', axis=0, tiled=True)  16.2 us
    all_gather x1, blocking collectives, shards(): lax.all_gather(hidden_share, 'rep', axis=0, tiled=True)  14.8 us
    dot_general x1, local copies, waits for them, and re-layouts, shards(): jnp.einsum('jkab,jkaf->jkbf', own_tiles, picked_up, preferred_element_typ...  12.8 us
    dot_general x1, matrix products, shards(): jnp.einsum('jkab,jkaf->jkbf', own_tiles, picked_up, preferred_element_typ...  11.6 us
  transfers between devices with their start and end apart: 6, of which 6 were waited for; matrix products, arithmetic and copies ran while one was open for 3% of the time, Pallas kernels for 0%

commit v1 on v0

--- a/solution.py
+++ b/solution.py
@@ -64,7 +64,11 @@
         jnp.bfloat16
     )
     hidden_share, grad_part, upstream_share = (out_rows, grad_part, up_rows)
-    weight_grad = lax.psum(grad_part, ("section", "rep")) * grad_scale
+
+    def _fix_keys(mine_x):
+        return jnp.sum(lax.all_gather(mine_x, ("section", "rep")), axis=0)
+
+    weight_grad = _fix_keys(grad_part) * grad_scale
     hidden, upstream = (
         lax.all_gather(hidden_share, "rep", axis=0, tiled=True),
         lax.all_gather(upstream_share, "rep", axis=0, tiled=True),

time: 488 us -> 421 us (0.86)
  waiting for transfers between devices: 338 us -> 263 us
  blocking collectives: 31 us -> 38.2 us
    psum x1 -> x0, waiting for transfers between devices: 107 us -> none  [shards(): weight_grad = lax.psum(grad_part, ('section', 'rep')) * grad_scale]
    all_gather x0 -> x1, waiting for transfers between devices: none -> 53 us  [_fix_keys(): return jnp.sum(lax.all_gather(mine_x, ('section', 'rep')), axis=0)]
    psum x3, waiting for transfers between devices: 152 us -> 130 us  [spread(): return lax.psum(kept, axis)]
    all_gather x1, blocking collectives: 14.8 us -> 22 us  [shards(): lax.all_gather(hidden_share, 'rep', axis=0, tiled=True)]
  transfers between devices with their start and end apart: 6 -> 6, of which waited for: 6 -> 6; matrix products, arithmetic and copies ran while one was open for 3% -> 4% of each run, Pallas kernels for 0% -> 0%
where the time goes in v1:
time: 421 us; the launch traced here: 420 us
  waiting for transfers between devices  263 us (62%)
  local copies, waits for them, and re-layouts  49.3 us (12%)
  matrix products  40.4 us (10%)
  blocking collectives  38.2 us (9%)
  between operations  15.8 us (4%)
  other arithmetic  13.2 us (3%)
    psum x3, waiting for transfers between devices, spread(): return lax.psum(kept, axis)  130 us
    psum x1, waiting for transfers between devices, shards(): lax.psum(contrib.astype(jnp.bfloat16), 'section').astype(jnp.float32)  54.2 us
    all_gather x1, waiting for transfers between devices, _fix_keys(): return jnp.sum(lax.all_gather(mine_x, ('section', 'rep')), axis=0)  53 us
    reduce_scatter x1, waiting for transfers between devices, shards(): lax.psum_scatter(partial_sum, 'rep', scatter_dimension=0, tiled=True)  25.6 us
    all_gather x1, blocking collectives, shards(): lax.all_gather(hidden_share, 'rep', axis=0, tiled=True)  22 us
    all_gather x1, blocking collectives, shards(): lax.all_gather(upstream_share, 'rep', axis=0, tiled=True)  16.2 us
    dot_general x1, local copies, waits for them, and re-layouts, shards(): jnp.einsum('jkab,jkaf->jkbf', own_tiles, picked_up, preferred_element_typ...  12.8 us
    dot_general x1, matrix products, shards(): jnp.einsum('jkab,jkaf->jkbf', own_tiles, picked_up, preferred_element_typ...  11.6 us
  transfers between devices with their start and end apart: 6, of which 6 were waited for; matrix products, arithmetic and copies ran while one was open for 4% of the time, Pallas kernels for 0%

profile of v1, /device:TPU:0, one launch (start us, length us, event | category | flops | bytes accessed | tf_op | source)
XLA Modules:
  0.0 420.0 jit_solution(7098529603962226911)
XLA Ops:
  9.5 6.2 %gather_fusion.1 = bf16[2048,128]{1,0:T(8,128)(2,1)S(1)} fusion(bf16[2048,128]{1,0:T(8,128)(2,1)S(1)} %copy-done, s32[2048]{0:T(1024)S(1)} %get-tuple-element.296), kind=kCustom, calls=%fused_computation.1 | custom fusion | bytes 1056768 | tf_op jit(solution)/shard_map/jit(_take)/gather | solution.py:30
  16.0 147.6 %while.16 = (s32[]{:T(128)}, f32[16,128,128]{2,0,1:T(8,128)S(1)}, s32[2,96]{1,0:T(2,128)}, s32[2]{0:T(128)}, bf16[2,96,128,128]{3,2,1,0:T(8,128)(2,1)}, /*index=...) while((s32[]{:T(128)}, f32[16,128,128]{2,0,1:T(8,128)S(1)}, ...), condition=%wide.region_2.3_spmd.clone, body=%wide.region_0.0_spmd.clone.sunk | while | flops 707269568 | bytes 31465112 | solution.py:48
  16.1 0.8 broadcast_select_fusion.3
  18.3 1.2 dynamic_slice.80
  20.9 57.2 %all-reduce.8.cloned.1.call-done = bf16[16,128,128]{2,1,0:T(8,128)(2,1)} async-done(((bf16[16,128,128]{2,1,0:T(8,128)(2,1)}), bf16[16,128,128]{2,1,0:T(8,128)(2,1)}) %all-reduce.8.cloned.1.call-update) | async-done | bytes 524304 | tf_op jit(solution)/shard_map/while/body/eval_jaxpr/psum | solution.py:10
  78.1 3.7 gather_fusion
  81.9 3.9 fusion.65
  85.8 5.7 %fusion.67 = f32[16,128,128]{2,0,1:T(8,128)S(1)} fusion(f32[96,128,128]{2,1,0:T(8,128)S(1)} %fusion.65, f32[16,128,128]{2,0,1:T(8,128)S(1)} %get-tuple-element.360, pred[]{:T(512)S(6)} %compare.6, s32[96]{0:T(128)S(1)} %fusion.66, pred[96]{0:T(512)(128)(4,1)S(1)} %iota_compare_fusion.5), kind=kOutput, calls=%fused_computation.14.clone.1 | convolution fusion | flops 302517248 | bytes 8389089 | tf_op jit(solution)/shard_map/while/body/eval_jaxpr/pk,kaf->paf/dot_general | solution.py:44
  91.6 0.8 broadcast_select_fusion.3
  93.8 1.2 dynamic_slice.80
  96.4 53.8 %all-reduce.8.cloned.1.call-done = bf16[16,128,128]{2,1,0:T(8,128)(2,1)} async-done(((bf16[16,128,128]{2,1,0:T(8,128)(2,1)}), bf16[16,128,128]{2,1,0:T(8,128)(2,1)}) %all-reduce.8.cloned.1.call-update) | async-done | bytes 524304 | tf_op jit(solution)/shard_map/while/body/eval_jaxpr/psum | solution.py:10
  150.2 3.7 gather_fusion
  154.0 3.9 fusion.65
  157.9 5.7 %fusion.67 = f32[16,128,128]{2,0,1:T(8,128)S(1)} fusion(f32[96,128,128]{2,1,0:T(8,128)S(1)} %fusion.65, f32[16,128,128]{2,0,1:T(8,128)S(1)} %get-tuple-element.360, pred[]{:T(512)S(6)} %compare.6, s32[96]{0:T(128)S(1)} %fusion.66, pred[96]{0:T(512)(128)(4,1)S(1)} %iota_compare_fusion.5), kind=kOutput, calls=%fused_computation.14.clone.1 | convolution fusion | flops 302517248 | bytes 8389089 | tf_op jit(solution)/shard_map/while/body/eval_jaxpr/pk,kaf->paf/dot_general | solution.py:44
  163.7 1.3 copy.11
  167.3 25.6 %reduce-scatter.2.cloned.1.call-done = f32[512,128]{1,0:T(8,128)} async-done(((f32[2048,128]{1,0:T(8,128)}), f32[512,128]{1,0:T(8,128)}) %reduce-scatter.2.cloned.1.call-update) | async-done | bytes 262160 | tf_op jit(solution)/shard_map/reduce_scatter | solution.py:53
  192.9 1.3 multiply_convert_fusion
  194.3 16.2 %all_gather.15 = bf16[2048,128]{1,0:T(8,128)(2,1)S(1)} all-gather(bf16[512,128]{1,0:T(8,128)(2,1)S(1)} %convolution_convert_fusion), channel_id=1, replica_groups=mesh['section'=8,'rep'=4] {'rep'}, dimensions={0}, use_global_device_ids=true | all-gather | bytes 655360 | tf_op jit(solution)/shard_map/all_gather | solution.py:74
  210.5 8.0 %gather_fusion.2 = bf16[192,128,128]{2,1,0:T(8,128)(2,1)} fusion(bf16[16,128,128]{2,1,0:T(8,128)(2,1)S(1)} %bitcast.61, s32[1024]{0:T(1024)S(1)} %pad_clamp_fusion.1), kind=kCustom, calls=%fused_computation.2 | custom fusion | bytes 12583680 | tf_op jit(solution)/shard_map/jit(_take)/gather | solution.py:77
  218.5 11.6 %fusion.26 = f32[2,96,128,128]{3,2,1,0:T(8,128)} fusion(bf16[2,96,128,128]{3,2,1,0:T(8,128)(2,1)} %bitcast.65, pred[2,96]{1,0:T(4,128)(4,1)S(1)} %compare_and_fusion.2, bf16[1,1,2,96,128,128]{5,4,3,2,1,0:T(8,128)(2,1)} %bitcast.63), kind=kOutput, calls=%fused_computation.34 | convolution fusion | flops 808452096 | bytes 25166016 | tf_op jit(solution)/shard_map/jkab,jkaf->jkbf/dot_general | solution.py:80
  230.1 12.8 %copy.14 = f32[2,96,128,128]{2,1,3,0:T(8,128)} copy(f32[2,96,128,128]{3,2,1,0:T(8,128)} %fusion.26) | data formatting | bytes 25165824 | tf_op jit(solution)/shard_map/jkab,jkaf->jkbf/dot_general | solution.py:80
  242.8 7.2 %fusion.30 = bf16[2,16,128,128]{3,1,2,0:T(8,128)(2,1)S(1)} fusion(f32[2,96,128,128]{2,1,3,0:T(8,128)} %copy.14, s32[2,96]{1,0:T(2,128)S(1)} %copy-done.3, pred[2,96]{1,0:T(4,128)(4,1)S(1)} %iota_compare_fusion.3), kind=kOutput, calls=%fused_computation.38 | convolution fusion | flops 604510208 | bytes 13632448 | tf_op jit(solution)/shard_map/jpk,jkbf->jpbf/dot_general | solution.py:87
  250.1 1.3 copy.12
  251.5 54.2 %all-reduce.4.cloned.1.call-done = bf16[2,2048,128]{2,1,0:T(8,128)(2,1)} async-done(((bf16[2,2048,128]{2,1,0:T(8,128)(2,1)}), bf16[2,2048,128]{2,1,0:T(8,128)(2,1)}) %all-reduce.4.cloned.1.call-update) | async-done | bytes 1048592 | tf_op jit(solution)/shard_map/psum | solution.py:92
  305.8 1.9 fusion.34
  307.8 0.9 fusion.37
  308.7 22.0 %all_gather.12 = bf16[2048,128]{1,0:T(8,128)(2,1)S(1)} all-gather(bf16[512,128]{1,0:T(8,128)(2,1)S(1)} %get-tuple-element.294), channel_id=1, replica_groups=mesh['section'=8,'rep'=4] {'rep'}, dimensions={0}, use_global_device_ids=true | all-gather | bytes 655360 | tf_op jit(solution)/shard_map/all_gather | solution.py:73
  330.7 18.7 %all-reduce.6.cloned.1.call-done = bf16[2048,128]{1,0:T(8,128)(2,1)} async-done(((bf16[2048,128]{1,0:T(8,128)(2,1)}), bf16[2048,128]{1,0:T(8,128)(2,1)}) %all-reduce.6.cloned.1.call-update) | async-done | bytes 524304 | tf_op jit(solution)/shard_map/psum | solution.py:10
  349.4 6.8 %scatter_custom_fusion = bf16[2048,128]{1,0:T(8,128)(2,1)} fusion(s32[2048]{0:T(1024)S(1)} %get-tuple-element.295, bf16[2048,128]{1,0:T(8,128)(2,1)} %all-reduce.6.cloned.1.call-done, bf16[]{:T(256)} %constant.191.clone.1), kind=kCustom, calls=%fused_computation.44 | custom fusion | bytes 524800 | tf_op jit(solution)/shard_map/scatter | solution.py:97
  356.2 53.0 %all-gather.3.cloned.1.call-done = f32[4096,128]{1,0:T(8,128)} async-done(((f32[128,128]{1,0:T(8,128)}), f32[4096,128]{1,0:T(8,128)}) %all-gather.3.cloned.1.call-update) | async-done | bytes 2097168 | tf_op jit(solution)/shard_map/all_gather | solution.py:69
  409.3 1.7 reduce_sum.9
  411.6 0.8 copy.32
  (41 shorter events, 10.6 us)
Async XLA Ops:
  8.0 1.5 copy-start
  16.0 176.9 %copy-start.2 = (bf16[128,128]{1,0:T(8,128)(2,1)S(1)}, bf16[128,128]{1,0:T(8,128)(2,1)}, u32[]{:S(2)}) copy-start(bf16[128,128]{1,0:T(8,128)(2,1)} %param.16) | copy-start | bytes 98308
  16.0 62.1 %all-reduce.8.cloned.1.call-start = ((), (), s32[]{:S(2)}) async-start(), calls=%async_computation.5 | async-start | bytes 1048576 | tf_op jit(solution)/shard_map/while/body/eval_jaxpr/psum | solution.py:10
  91.5 58.7 %all-reduce.8.cloned.1.call-start = ((), (), s32[]{:S(2)}) async-start(), calls=%async_computation.5 | async-start | bytes 1048576 | tf_op jit(solution)/shard_map/while/body/eval_jaxpr/psum | solution.py:10
  163.6 29.2 %reduce-scatter.2.cloned.1.call-start = ((), (), s32[]{:S(2)}) async-start(), calls=%async_computation.1 | async-start | bytes 1310720 | tf_op jit(solution)/shard_map/reduce_scatter | solution.py:53
  165.0 140.7 %all-reduce.4.cloned.1.call-start = ((), (), s32[]{:S(2)}) async-start(), calls=%async_computation.2 | async-start | bytes 2097152 | tf_op jit(solution)/shard_map/psum | solution.py:92
  230.1 12.8 %copy-start.3 = (s32[2,96]{1,0:T(2,128)S(1)}, s32[2,96]{1,0:T(2,128)}, u32[]{:S(2)}) copy-start(s32[2,96]{1,0:T(2,128)} %get-tuple-element.411) | copy-start | bytes 2308
  242.8 64.9 %copy-start.1 = (f32[512,128]{1,0:T(8,128)S(1)}, f32[512,128]{1,0:T(8,128)}, u32[]{:S(2)}) copy-start(f32[512,128]{1,0:T(8,128)} %reduce-scatter.2.cloned.1.call-done) | copy-start | bytes 786436
  251.4 98.0 %all-reduce.6.cloned.1.call-start = ((), (), s32[]{:S(2)}) async-start(), calls=%async_computation.3 | async-start | bytes 1048576 | tf_op jit(solution)/shard_map/psum | solution.py:10
  307.7 101.6 %all-gather.3.cloned.1.call-start = ((), (), s32[]{:S(2)}) async-start(), calls=%async_computation.4 | async-start | bytes 2162688 | tf_op jit(solution)/shard_map/all_gather | solution.py:69
Sparse Core Ops, SparseCore 0:
  20.8 57.2 all-reduce.7
  96.3 53.8 all-reduce.7
Sparse Core Ops, SparseCore 1:
  166.4 26.4 reduce-scatter.1
  251.5 54.2 all-reduce.3
  308.7 40.7 all-reduce.5
  353.4 55.9 all-gather.2
